TPU v7x, 32 devices: a whole 2x2x4 slice. The times are simulated.
32 devices in a mesh: wide: 8 (over z, y), narrow: 4 (over x, core).
Axes of the slice: x: 2, y: 2, z: 4, core: 2. Of those that a mesh axis runs over, the one named last changes fastest.
Arguments:
- tokens: bfloat16 [64, 600, 768], P(('wide', 'narrow')), may hold values from -6 to 6
- lengths: int32 [64], P(('wide', 'narrow')), may hold values from 256 to 600, as said below
- blocks: int32 [64, 600], P(('wide', 'narrow')), may hold values from 0 to 4, never falling along the last dimension, each value on 1 to 300 neighbouring positions
- ln1_gain: bfloat16 [768], P(('wide', 'narrow')), may hold values from 0.25 to 1.75
- ln1_bias: bfloat16 [768], P(('wide', 'narrow')), may hold values from -1.75 to 1.75
- qkv_weight: bfloat16 [768, 2304], P(('wide', 'narrow')), may hold values from -0.3125 to 0.3125
- qv_bias: bfloat16 [1536], P(('wide', 'narrow')), may hold values from -1.75 to 1.75
- out_weight: bfloat16 [768, 768], P(('wide', 'narrow')), may hold values from -1.25 to 1.25
- out_bias: bfloat16 [768], P(('wide', 'narrow')), may hold values from -1.75 to 1.75
- ln2_gain: bfloat16 [768], P(('wide', 'narrow')), may hold values from 0.25 to 1.75
- ln2_bias: bfloat16 [768], P(('wide', 'narrow')), may hold values from -1.75 to 1.75
- up_weight: bfloat16 [768, 3072], P(('wide', 'narrow')), may hold values from -0.21875 to 0.21875
- up_bias: bfloat16 [3072], P(('wide', 'narrow')), may hold values from -1.75 to 1.75
- down_weight: bfloat16 [3072, 768], P(('wide', 'narrow')), may hold values from -0.109375 to 0.109375
- down_bias: bfloat16 [768], P(('wide', 'narrow')), may hold values from -1.75 to 1.75
- cotangent: bfloat16 [64, 600, 768], P(('wide', 'narrow')), may hold values from -12 to 12
Outputs:
- output: bfloat16 [64, 600, 768], P(('wide', 'narrow'))
- input_grad: float32 [64, 600, 768], P(('wide', 'narrow'))
- ln1_gain_grad: float32 [768], P(('wide', 'narrow'))
- ln1_bias_grad: float32 [768], P(('wide', 'narrow'))
- qkv_weight_grad: float32 [768, 2304], P(('wide', 'narrow'))
- qv_bias_grad: float32 [1536], P(('wide', 'narrow'))
- out_weight_grad: float32 [768, 768], P(('wide', 'narrow'))
- out_bias_grad: float32 [768], P(('wide', 'narrow'))
- ln2_gain_grad: float32 [768], P(('wide', 'narrow'))
- ln2_bias_grad: float32 [768], P(('wide', 'narrow'))
- up_weight_grad: float32 [768, 3072], P(('wide', 'narrow'))
- up_bias_grad: float32 [3072], P(('wide', 'narrow'))
- down_weight_grad: float32 [3072, 768], P(('wide', 'narrow'))
- down_bias_grad: float32 [768], P(('wide', 'narrow'))
Inputs may be any that keep to these rules, and one draw needn't show every extreme that they name: Slots at and after lengths[b] of item b are padding; some item has 600 real tokens and some 256. `blocks`: block ids of an item start at 0 at slot 0 and never fall along the slots.
All inputs are finite; a program needn't handle non-finite values.
Results may differ from a plain program's by a relative error of at most 0.012.
The roundings to bfloat16 on the way count: a program that leaves them out, or rounds other values in their place, can miss the bound.
Values may be sent and summed in bfloat16 or wider, within the bound.
No kernel may reach another device: no remote copies, remote signals or barrier semaphores. Data moves between devices by JAX's collectives and lax.ppermute only.
A program may use at most 256 MiB of HBM per device.

v0:
```python
from functools import partial
import jax
import jax.numpy as jnp
from jax import lax
from jax.sharding import PartitionSpec as P

D = 768
HEADS = 12
HEAD = 64
norm_epsilon = 1e-05
masked_score = -1e30


def layer_norm(values, gain, shift):
    centred = values - jnp.mean(values, axis=-1, keepdims=True)
    inverse = lax.rsqrt(jnp.mean(centred * centred, axis=-1, keepdims=True) + norm_epsilon)
    scaled = centred * inverse
    return (scaled * gain + shift, scaled, inverse)


def norm_back(d_normed, scaled, inverse, gain):
    gain_grad = jnp.sum(d_normed * scaled, axis=0)
    shift_grad = jnp.sum(d_normed, axis=0)
    d_scaled = d_normed * gain
    centre_term = jnp.mean(d_scaled, axis=-1, keepdims=True)
    slope_term = jnp.mean(d_scaled * scaled, axis=-1, keepdims=True)
    return (inverse * (d_scaled - centre_term - scaled * slope_term), gain_grad, shift_grad)


def allowed_pairs(item_length, block_ids):
    slot_count = block_ids.shape[0]
    column = lax.broadcasted_iota(jnp.int32, (slot_count, slot_count), 1)
    return (block_ids[None, :] <= block_ids[:, None]) & (column < item_length)


def head_split(packed, index):
    slot_count = packed.shape[0]
    return packed[:, index * D : (index + 1) * D].reshape(slot_count, HEADS, HEAD)


def score_table(queries, key_rows, allowed):
    scores = jnp.einsum(
        "qhd,khd->hqk", queries, key_rows, preferred_element_type=jnp.float32
    ) * HEAD ** (-0.5)
    return jnp.where(allowed[None], scores, masked_score)


def attend_forward(packed):
    qkv_item, item_length, block_ids = packed
    slot_count = qkv_item.shape[0]
    scores = score_table(
        head_split(qkv_item, 0), head_split(qkv_item, 1), allowed_pairs(item_length, block_ids)
    )
    peak_score = jnp.max(scores, axis=-1, keepdims=True)
    exponent = jnp.exp(scores - peak_score)
    row_total = jnp.sum(exponent, axis=-1, keepdims=True)
    probs_low = (exponent / row_total).astype(jnp.bfloat16)
    mixed_heads = jnp.einsum(
        "hqk,khd->qhd", probs_low, head_split(qkv_item, 2), preferred_element_type=jnp.float32
    )
    return (
        mixed_heads.reshape(slot_count, D).astype(jnp.bfloat16),
        peak_score + jnp.log(row_total),
    )


def attend_backward(packed):
    qkv_item, item_length, block_ids, log_total, d_mixed = packed
    slot_count = qkv_item.shape[0]
    queries = head_split(qkv_item, 0)
    key_rows = head_split(qkv_item, 1)
    value_rows = head_split(qkv_item, 2)
    scores = score_table(queries, key_rows, allowed_pairs(item_length, block_ids))
    probs = jnp.exp(scores - log_total)
    probs_low = probs.astype(jnp.bfloat16)
    d_heads = d_mixed.reshape(slot_count, HEADS, HEAD)
    d_values = jnp.einsum("hqk,qhd->khd", probs_low, d_heads, preferred_element_type=jnp.float32)
    d_probs = jnp.einsum("qhd,khd->hqk", d_heads, value_rows, preferred_element_type=jnp.float32)
    d_scores = (probs * (d_probs - jnp.sum(probs * d_probs, axis=-1, keepdims=True))).astype(
        jnp.bfloat16
    )
    d_queries = jnp.einsum(
        "hqk,khd->qhd", d_scores, key_rows, preferred_element_type=jnp.float32
    ) * HEAD ** (-0.5)
    d_keys = jnp.einsum(
        "hqk,qhd->khd", d_scores, queries, preferred_element_type=jnp.float32
    ) * HEAD ** (-0.5)
    joined = jnp.concatenate(
        [
            d_queries.reshape(slot_count, D),
            d_keys.reshape(slot_count, D),
            d_values.reshape(slot_count, D),
        ],
        axis=1,
    )
    return joined.astype(jnp.bfloat16)


def fetch(shards):
    (
        gain_one,
        shift_one,
        w_qkv,
        bias_qv,
        w_out,
        bias_out,
        gain_two,
        shift_two,
        w_up,
        bias_up,
        w_down,
        bias_down,
    ) = shards
    whole_set = (
        lax.all_gather(gain_one, ("wide", "narrow"), axis=0, tiled=True),
        lax.all_gather(shift_one, ("wide", "narrow"), axis=0, tiled=True),
        lax.all_gather(w_qkv, ("wide", "narrow"), axis=0, tiled=True),
        lax.all_gather(bias_qv, ("wide", "narrow"), axis=0, tiled=True),
        lax.all_gather(w_out, ("wide", "narrow"), axis=0, tiled=True),
        lax.all_gather(bias_out, ("wide", "narrow"), axis=0, tiled=True),
        lax.all_gather(gain_two, ("wide", "narrow"), axis=0, tiled=True),
        lax.all_gather(shift_two, ("wide", "narrow"), axis=0, tiled=True),
        lax.all_gather(w_up, ("wide", "narrow"), axis=0, tiled=True),
        lax.all_gather(bias_up, ("wide", "narrow"), axis=0, tiled=True),
        lax.all_gather(w_down, ("wide", "narrow"), axis=0, tiled=True),
        lax.all_gather(bias_down, ("wide", "narrow"), axis=0, tiled=True),
    )
    return whole_set


def reduce_grads(grads):
    (
        gain_one,
        shift_one,
        w_qkv,
        bias_qv,
        w_out,
        bias_out,
        gain_two,
        shift_two,
        w_up,
        bias_up,
        w_down,
        bias_down,
    ) = grads
    owned = (
        lax.psum_scatter(gain_one, ("wide", "narrow"), scatter_dimension=0, tiled=True),
        lax.psum_scatter(shift_one, ("wide", "narrow"), scatter_dimension=0, tiled=True),
        lax.psum_scatter(w_qkv, ("wide", "narrow"), scatter_dimension=0, tiled=True),
        lax.psum_scatter(bias_qv, ("wide", "narrow"), scatter_dimension=0, tiled=True),
        lax.psum_scatter(w_out, ("wide", "narrow"), scatter_dimension=0, tiled=True),
        lax.psum_scatter(bias_out, ("wide", "narrow"), scatter_dimension=0, tiled=True),
        lax.psum_scatter(gain_two, ("wide", "narrow"), scatter_dimension=0, tiled=True),
        lax.psum_scatter(shift_two, ("wide", "narrow"), scatter_dimension=0, tiled=True),
        lax.psum_scatter(w_up, ("wide", "narrow"), scatter_dimension=0, tiled=True),
        lax.psum_scatter(bias_up, ("wide", "narrow"), scatter_dimension=0, tiled=True),
        lax.psum_scatter(w_down, ("wide", "narrow"), scatter_dimension=0, tiled=True),
        lax.psum_scatter(bias_down, ("wide", "narrow"), scatter_dimension=0, tiled=True),
    )
    return tuple(owned)


def body(
    tokens,
    lengths,
    blocks,
    ln1_gain,
    ln1_bias,
    qkv_weight,
    qv_bias,
    out_weight,
    out_bias,
    ln2_gain,
    ln2_bias,
    up_weight,
    up_bias,
    down_weight,
    down_bias,
    cotangent,
):
    item_count, slot_count, model_width = tokens.shape
    row_count = item_count * slot_count
    shards = (
        ln1_gain,
        ln1_bias,
        qkv_weight,
        qv_bias,
        out_weight,
        out_bias,
        ln2_gain,
        ln2_bias,
        up_weight,
        up_bias,
        down_weight,
        down_bias,
    )
    layer_weights = fetch(shards)
    (
        gain_one,
        shift_one,
        w_qkv,
        bias_qv,
        w_out,
        bias_out,
        gain_two,
        shift_two,
        w_up,
        bias_up,
        w_down,
        bias_down,
    ) = layer_weights
    inputs = tokens.reshape(row_count, model_width).astype(jnp.float32)
    normed_one, scaled_one, inverse_one = layer_norm(
        inputs, gain_one.astype(jnp.float32), shift_one.astype(jnp.float32)
    )
    normed_one = normed_one.astype(jnp.bfloat16)
    qv_float = bias_qv.astype(jnp.float32)
    bias_full = jnp.concatenate(
        [qv_float[:model_width], jnp.zeros((model_width,), jnp.float32), qv_float[model_width:]]
    )
    qkv_low = (jnp.dot(normed_one, w_qkv, preferred_element_type=jnp.float32) + bias_full).astype(
        jnp.bfloat16
    )
    qkv_items = qkv_low.reshape(item_count, slot_count, 3 * model_width)
    mixed_items, log_totals = lax.map(attend_forward, (qkv_items, lengths, blocks))
    mixed_low = mixed_items.reshape(row_count, model_width)
    middle = (
        inputs
        + jnp.dot(mixed_low, w_out, preferred_element_type=jnp.float32)
        + bias_out.astype(jnp.float32)
    )
    normed_two, scaled_two, inverse_two = layer_norm(
        middle, gain_two.astype(jnp.float32), shift_two.astype(jnp.float32)
    )
    normed_two = normed_two.astype(jnp.bfloat16)
    pre_active = jnp.dot(normed_two, w_up, preferred_element_type=jnp.float32) + bias_up.astype(
        jnp.float32
    )
    active, gelu_back = jax.vjp(partial(jax.nn.gelu, approximate=True), pre_active)
    active_low = active.astype(jnp.bfloat16)
    branch_mlp = jnp.dot(active_low, w_down, preferred_element_type=jnp.float32) + bias_down.astype(
        jnp.float32
    )
    slot_ids = lax.broadcasted_iota(jnp.int32, (item_count, slot_count), 1)
    valid_rows = (slot_ids < lengths[:, None]).astype(jnp.float32).reshape(row_count, 1)
    output = (
        ((middle + branch_mlp) * valid_rows)
        .astype(jnp.bfloat16)
        .reshape(item_count, slot_count, model_width)
    )
    back_weights = fetch(shards)
    (
        back_gain_one,
        back_shift_one,
        back_qkv,
        back_bias_qv,
        back_out,
        back_bias_out,
        back_gain_two,
        back_shift_two,
        back_up,
        back_bias_up,
        back_down,
        back_bias_down,
    ) = back_weights
    d_result = cotangent.reshape(row_count, model_width).astype(jnp.float32) * valid_rows
    d_lower = d_result.astype(jnp.bfloat16)
    grad_bias_down = jnp.sum(d_lower.astype(jnp.float32), axis=0)
    grad_down = jnp.einsum("rf,rd->fd", active_low, d_lower, preferred_element_type=jnp.float32)
    d_active = jnp.einsum("rd,fd->rf", d_lower, back_down, preferred_element_type=jnp.float32)
    d_pre = gelu_back(d_active)[0].astype(jnp.bfloat16)
    grad_bias_up = jnp.sum(d_pre.astype(jnp.float32), axis=0)
    grad_up = jnp.einsum("rd,rf->df", normed_two, d_pre, preferred_element_type=jnp.float32)
    d_normed_two = jnp.einsum("rf,df->rd", d_pre, back_up, preferred_element_type=jnp.float32)
    d_inner, grad_gain_two, grad_shift_two = norm_back(
        d_normed_two, scaled_two, inverse_two, back_gain_two.astype(jnp.float32)
    )
    d_middle = d_result + d_inner
    d_branch = d_middle.astype(jnp.bfloat16)
    grad_bias_out = jnp.sum(d_branch.astype(jnp.float32), axis=0)
    grad_out = jnp.einsum("rd,re->de", mixed_low, d_branch, preferred_element_type=jnp.float32)
    d_mixed = jnp.einsum(
        "re,de->rd", d_branch, back_out, preferred_element_type=jnp.float32
    ).astype(jnp.bfloat16)
    d_qkv = lax.map(
        attend_backward,
        (
            qkv_items,
            lengths,
            blocks,
            log_totals,
            d_mixed.reshape(item_count, slot_count, model_width),
        ),
    )
    d_qkv = d_qkv.reshape(row_count, 3 * model_width)
    column_sums = jnp.sum(d_qkv.astype(jnp.float32), axis=0)
    grad_bias_qv = jnp.concatenate([column_sums[:model_width], column_sums[2 * model_width :]])
    grad_qkv = jnp.einsum("rd,re->de", normed_one, d_qkv, preferred_element_type=jnp.float32)
    d_normed_one = jnp.einsum("re,de->rd", d_qkv, back_qkv, preferred_element_type=jnp.float32)
    d_first, grad_gain_one, grad_shift_one = norm_back(
        d_normed_one, scaled_one, inverse_one, back_gain_one.astype(jnp.float32)
    )
    input_grad = (d_middle + d_first).reshape(item_count, slot_count, model_width)
    owned = reduce_grads(
        (
            grad_gain_one,
            grad_shift_one,
            grad_qkv,
            grad_bias_qv,
            grad_out,
            grad_bias_out,
            grad_gain_two,
            grad_shift_two,
            grad_up,
            grad_bias_up,
            grad_down,
            grad_bias_down,
        )
    )
    return (output, input_grad) + owned


def solution(mesh):
    return jax.shard_map(
        body,
        mesh=mesh,
        in_specs=(
            P(("wide", "narrow"), None, None),
            P(("wide", "narrow")),
            P(("wide", "narrow"), None),
            P(("wide", "narrow")),
            P(("wide", "narrow")),
            P(("wide", "narrow"), None),
            P(("wide", "narrow")),
            P(("wide", "narrow"), None),
            P(("wide", "narrow")),
            P(("wide", "narrow")),
            P(("wide", "narrow")),
            P(("wide", "narrow"), None),
            P(("wide", "narrow")),
            P(("wide", "narrow"), None),
            P(("wide", "narrow")),
            P(("wide", "narrow"), None, None),
        ),
        out_specs=(
            P(("wide", "narrow"), None, None),
            P(("wide", "narrow"), None, None),
            P(("wide", "narrow")),
            P(("wide", "narrow")),
            P(("wide", "narrow"), None),
            P(("wide", "narrow")),
            P(("wide", "narrow"), None),
            P(("wide", "narrow")),
            P(("wide", "narrow")),
            P(("wide", "narrow")),
            P(("wide", "narrow"), None),
            P(("wide", "narrow")),
            P(("wide", "narrow"), None),
            P(("wide", "narrow")),
        ),
        check_vma=False,
    )
```

profile of v0, /device:TPU:0, one launch (start us, length us, event | category | flops | bytes accessed | tf_op | source)
XLA Modules:
  0.0 839.9 jit_solution(17000271752070816200)
XLA Ops:
  12.1 2.2 multiply_reduce_fusion.6
  16.5 42.7 %all-reduce.17 = (bf16[1536]{0:T(1024)(128)(2,1)S(1)}, bf16[768]{0:T(1024)(128)(2,1)S(1)}, bf16[768]{0:T(1024)(128)(2,1)S(1)}, bf16[768]{0:T(1024)(128)(2,1)S(1)...) all-reduce(bf16[1536]{0:T(1024)(128)(2,1)S(1)} %dynamic-update-slic, ...), channel_id=1, replica_groups=mesh['wide'=8,'narrow'=4] {'wide','narrow'}, use_global_device_ids=true, to_apply=%add.2 | all-reduce | flops 9216 | bytes 36864
  61.7 3.2 fusion.27
  64.9 2.4 fusion.26
  67.3 6.6 all-gather.5.cloned.1.call-done
  73.9 10.0 %fusion.22 = bf16[1200,2304]{1,0:T(8,128)(2,1)} fusion(bf16[768,2304]{1,0:T(8,128)(2,1)} %all-gather.5.cloned.1.call-done, f32[2304]{0:T(1024)S(1)} %pad_maximum_fusion, f32[1200,768]{1,0:T(8,128)} %fusion.26, f32[768]{0:T(1024)S(1)} %convert_element_type.143, f32[768]{0:T(1024)S(1)} %convert_element_type.142), kind=kOutput, calls=%fused_computation.47 | convolution fusion | flops 4255027200 | bytes 12770304 | tf_op jit(solution)/shard_map/dot_general | solution.py:221
  83.9 8.8 %copy.52 = bf16[2,600,2304]{1,2,0:T(8,128)(2,1)} copy(bf16[2,600,2304]{2,1,0:T(8,128)(2,1)} %bitcast.156) | data formatting | bytes 11059200 | tf_op jit(solution)/shard_map/while | solution.py:225
  92.8 78.2 %while.22 = (s32[]{:T(128)}, bf16[2,600,768]{2,1,0:T(8,128)(2,1)}, f32[2,12,600,1]{2,1,3,0:T(8,128)S(1)}, bf16[2,600,2304]{1,2,0:T(8,128)(2,1)}, s32[2,600]{1,0:T(2,128)S(1)}, /*index=5*/s32[2]{0:T(128)S(1)}, s32[]{:T(128)}) while((s32[]{:T(128)}, bf16[2,600,768]{2,1,0:T(8,128)(2,1)}, f32[2,12,600,1]{2,1,3,0:T(8,128)S(1)}, ...), condition=%wide.region_5.6_spmd, body=%wide.region_2.5_spmd.sunk | while | flops 1158934144 | bytes 71987392 | solution.py:225
  94.8 2.1 dynamic-slice_bitcast_fusion.6
  98.1 8.2 fusion.99
  106.3 10.1 %fusion.100 = f32[12,600]{1,0:T(8,128)S(1)} fusion(f32[12,600,600]{1,2,0:T(8,128)} %get-tuple-element.288, f32[12,600]{1,0:T(8,128)S(1)} %get-tuple-element.289, pred[600,600]{0,1:T(8,128)(4,1)S(1)} %compare_and_fusion.4), kind=kLoop, calls=%fused_computation.4.clone.1 | loop fusion | flops 17272800 | bytes 17697600 | tf_op jit(solution)/shard_map/while/body/eval_jaxpr/reduce_sum | solution.py:56
  116.4 13.0 %fusion.101 = bf16[12,64,600]{2,1,0:T(8,128)(2,1)} fusion(bf16[600,12,64]{0,2,1:T(8,128)(2,1)} %bitcast.152, f32[12,600,600]{1,2,0:T(8,128)} %get-tuple-element.288, f32[12,600]{1,0:T(8,128)S(1)} %fusion.100, f32[12,600]{1,0:T(8,128)S(1)} %get-tuple-element.289, pred[600,600]{0,1:T(8,128)(4,1)S(1)} %compare_and_fusion.4), kind=kOutput, calls=%fused_computation.8.clone.1 | convolution fusion | flops 575020800 | bytes 19540800 | tf_op jit(solution)/shard_map/while/body/eval_jaxpr/hqk,khd->qhd/dot_general | solution.py:58
  136.9 8.2 fusion.99
  145.0 10.1 %fusion.100 = f32[12,600]{1,0:T(8,128)S(1)} fusion(f32[12,600,600]{1,2,0:T(8,128)} %get-tuple-element.288, f32[12,600]{1,0:T(8,128)S(1)} %get-tuple-element.289, pred[600,600]{0,1:T(8,128)(4,1)S(1)} %compare_and_fusion.4), kind=kLoop, calls=%fused_computation.4.clone.1 | loop fusion | flops 17272800 | bytes 17697600 | tf_op jit(solution)/shard_map/while/body/eval_jaxpr/reduce_sum | solution.py:56
  155.2 13.1 %fusion.101 = bf16[12,64,600]{2,1,0:T(8,128)(2,1)} fusion(bf16[600,12,64]{0,2,1:T(8,128)(2,1)} %bitcast.152, f32[12,600,600]{1,2,0:T(8,128)} %get-tuple-element.288, f32[12,600]{1,0:T(8,128)S(1)} %fusion.100, f32[12,600]{1,0:T(8,128)S(1)} %get-tuple-element.289, pred[600,600]{0,1:T(8,128)(4,1)S(1)} %compare_and_fusion.4), kind=kOutput, calls=%fused_computation.8.clone.1 | convolution fusion | flops 575020800 | bytes 19540800 | tf_op jit(solution)/shard_map/while/body/eval_jaxpr/hqk,khd->qhd/dot_general | solution.py:58
  171.0 3.7 fusion.45
  177.2 18.0 %all-gather.9.cloned.1.call-done = bf16[768,3072]{1,0:T(8,128)(2,1)} async-done(((bf16[24,3072]{1,0:T(8,128)(2,1)}), bf16[768,3072]{1,0:T(8,128)(2,1)}) %all-gather.9.cloned.1.call-update) | async-done | bytes 4718608 | tf_op jit(solution)/shard_map/all_gather | solution.py:123
  195.2 12.4 %convolution_add_fusion.1 = f32[1200,3072]{1,0:T(8,128)} fusion(bf16[768,3072]{1,0:T(8,128)(2,1)} %all-gather.9.cloned.1.call-done, f32[3072]{0:T(1024)S(1)} %copy-done.35, f32[1200,768]{1,0:T(8,128)} %copy-done.5, f32[768]{0:T(1024)S(1)} %copy-done.37, f32[768]{0:T(1024)S(1)} %copy-done.32, f32[1200]{0:T(1024)S(1)} %add_rsqrt_fusion, ...), kind=kOutput, calls=%fused_computation.45 | convolution fusion | flops 5670604800 | bytes 23178624 | tf_op jit(solution)/shard_map/dot_general | solution.py:236
  207.6 52.9 %all-gather.11.cloned.1.call-done = bf16[3072,768]{1,0:T(8,128)(2,1)} async-done(((bf16[96,768]{1,0:T(8,128)(2,1)}), bf16[3072,768]{1,0:T(8,128)(2,1)}) %all-gather.11.cloned.1.call-update) | async-done | bytes 4718608 | tf_op jit(solution)/shard_map/all_gather | solution.py:125
  260.4 18.6 %convert_reduce_fusion = (f32[3072]{0:T(1024)}, bf16[1200,3072]{1,0:T(8,128)(2,1)}) fusion(f32[1200,3072]{1,0:T(8,128)} %convolution_add_fusion.1, bf16[1200,768]{1,0:T(8,128)(2,1)S(1)} %copy-done.10, bf16[3072,768]{1,0:T(8,128)(2,1)} %all-gather.11.cloned.1.call-done), kind=kOutput, calls=%fused_computation.42 | convolution fusion | flops 5743408128 | bytes 28692480 | tf_op jit(solution)/shard_map/rd,fd->rf/dot_general | solution.py:270
  279.1 10.6 %multiply_reduce_fusion.1 = (f32[768]{0:T(1024)}, f32[1200]{0:T(1024)S(1)}, f32[1200]{0:T(1024)S(1)}, f32[768]{0:T(1024)}, f32[1200,768]{1,0:T(8,128)S(1)}) fusion(f32[1200,768]{1,0:T(8,128)S(1)} %copy-done.6, f32[1200]{0:T(1024)S(1)} %add_rsqrt_fusion, f32[1200]{0:T(1024)S(1)} %broadcast_multiply_fusion.4, f32[768]{0:T(1024)S(1)} %copy-done.32, ...), kind=kOutput, calls=%fused_computation.59 | convolution fusion | flops 5670600704 | bytes 19492608 | tf_op jit(solution)/shard_map/rf,df->rd/dot_general | solution.py:274
  289.7 2.3 convert_reduce_fusion.3
  293.9 3.2 fusion.35
  297.2 4.9 convolution_convert_fusion
  302.2 116.2 %while.23 = (s32[]{:T(128)}, bf16[2,600,2304]{1,2,0:T(8,128)(2,1)}, bf16[2,600,2304]{1,2,0:T(8,128)(2,1)}, s32[2,600]{1,0:T(2,128)S(1)}, s32[2]{0:T(128)S(1)}, /...) while((s32[]{:T(128)}, bf16[2,600,2304]{1,2,0:T(8,128)(2,1)}, ...), condition=%wide.region_12.13_spmd, body=%wide.region_10.12_spmd.sunk | while | flops 2840911872 | bytes 160925648 | solution.py:285
  306.1 2.1 dynamic-slice_bitcast_fusion.7
  308.5 8.2 fusion.113
  316.7 11.0 %fusion.114 = bf16[12,64,600]{2,1,0:T(8,128)(2,1)S(1)} fusion(bf16[600,12,64]{0,2,1:T(8,128)(2,1)S(1)} %bitcast.148, f32[12,600,600]{1,2,0:T(8,128)} %fusion.113, f32[12,600]{1,0:T(8,128)S(1)} %dynamic-slice_bitcast_fusion.8, pred[600,600]{0,1:T(8,128)(4,1)S(1)} %compare_and_fusion.5), kind=kOutput, calls=%fused_computation.26.clone.1 | convolution fusion | flops 570700800 | bytes 19512000 | tf_op jit(solution)/shard_map/while/body/eval_jaxpr/hqk,qhd->khd/dot_general | solution.py:77
  327.7 13.2 %multiply_reduce_fusion.10 = (f32[12,600]{1,0:T(8,128)S(1)}, f32[12,600,600]{1,2,0:T(8,128)}) fusion(f32[12,600,600]{1,2,0:T(8,128)} %fusion.113, f32[12,600]{1,0:T(8,128)S(1)} %dynamic-slice_bitcast_fusion.8, pred[600,600]{0,1:T(8,128)(4,1)S(1)} %compare_and_fusion.5, bf16[600,12,64]{0,2,1:T(8,128)(2,1)S(1)} %bitcast.149, ...), kind=kOutput, calls=%fused_computation.16.clone.1 | convolution fusion | flops 574552832 | bytes 36820800 | tf_op jit(solution)/shard_map/while/body/eval_jaxpr/qhd,khd->hqk/dot_general | solution.py:78
  340.9 13.4 %multiply_convert_fusion.10 = bf16[12,600,600]{1,2,0:T(8,128)(2,1)S(1)} fusion(f32[12,600,600]{1,2,0:T(8,128)} %get-tuple-element.300, f32[12,600,600]{1,2,0:T(8,128)} %fusion.113, f32[12,600]{1,0:T(8,128)S(1)} %get-tuple-element.301, f32[12,600]{1,0:T(8,128)S(1)} %dynamic-slice_bitcast_fusion.8, pred[600,600]{0,1:T(8,128)(4,1)S(1)} %compare_and_fusion.5), kind=kLoop, calls=%fused_computation.15.clone.1 | loop fusion | flops 25920000 | bytes 43617600 | tf_op jit(solution)/shard_map/while/body/eval_jaxpr/convert_element_type | solution.py:79
  356.0 2.8 multiply_convert_fusion.11
  364.3 2.1 dynamic-slice_bitcast_fusion.7
  366.6 8.1 fusion.113
  374.7 10.8 %fusion.114 = bf16[12,64,600]{2,1,0:T(8,128)(2,1)S(1)} fusion(bf16[600,12,64]{0,2,1:T(8,128)(2,1)S(1)} %bitcast.148, f32[12,600,600]{1,2,0:T(8,128)} %fusion.113, f32[12,600]{1,0:T(8,128)S(1)} %dynamic-slice_bitcast_fusion.8, pred[600,600]{0,1:T(8,128)(4,1)S(1)} %compare_and_fusion.5), kind=kOutput, calls=%fused_computation.26.clone.1 | convolution fusion | flops 570700800 | bytes 19512000 | tf_op jit(solution)/shard_map/while/body/eval_jaxpr/hqk,qhd->khd/dot_general | solution.py:77
  385.6 13.1 %multiply_reduce_fusion.10 = (f32[12,600]{1,0:T(8,128)S(1)}, f32[12,600,600]{1,2,0:T(8,128)}) fusion(f32[12,600,600]{1,2,0:T(8,128)} %fusion.113, f32[12,600]{1,0:T(8,128)S(1)} %dynamic-slice_bitcast_fusion.8, pred[600,600]{0,1:T(8,128)(4,1)S(1)} %compare_and_fusion.5, bf16[600,12,64]{0,2,1:T(8,128)(2,1)S(1)} %bitcast.149, ...), kind=kOutput, calls=%fused_computation.16.clone.1 | convolution fusion | flops 574552832 | bytes 36820800 | tf_op jit(solution)/shard_map/while/body/eval_jaxpr/qhd,khd->hqk/dot_general | solution.py:78
  398.7 13.0 %multiply_convert_fusion.10 = bf16[12,600,600]{1,2,0:T(8,128)(2,1)S(1)} fusion(f32[12,600,600]{1,2,0:T(8,128)} %get-tuple-element.300, f32[12,600,600]{1,2,0:T(8,128)} %fusion.113, f32[12,600]{1,0:T(8,128)S(1)} %get-tuple-element.301, f32[12,600]{1,0:T(8,128)S(1)} %dynamic-slice_bitcast_fusion.8, pred[600,600]{0,1:T(8,128)(4,1)S(1)} %compare_and_fusion.5), kind=kLoop, calls=%fused_computation.15.clone.1 | loop fusion | flops 25920000 | bytes 43617600 | tf_op jit(solution)/shard_map/while/body/eval_jaxpr/convert_element_type | solution.py:79
  413.4 2.8 multiply_convert_fusion.11
  418.4 11.7 %convolution_bitcast_fusion = f32[768,2304]{1,0:T(8,128)} fusion(bf16[2,600,2304]{1,2,0:T(8,128)(2,1)} %get-tuple-element.86, bf16[2,600,768]{2,1,0:T(8,128)(2,1)} %param.20, f32[768]{0:T(1024)S(1)} %copy-done.40, f32[768]{0:T(1024)S(1)} %copy-done.31, f32[2,600]{1,0:T(2,128)S(1)} %copy-done.29, f32[2,600]{1,0:T(2,128)S(1)} %copy-done.25), kind=kOutput, calls=%fused_computation.48 | convolution fusion | flops 4252262400 | bytes 14466432 | tf_op jit(solution)/shard_map/rd,re->de/dot_general | solution.py:298
  431.6 13.5 %fusion.39 = f32[3072,768]{1,0:T(8,128)} fusion(bf16[1200,768]{1,0:T(8,128)(2,1)S(1)} %copy-done.11, f32[1200,3072]{1,0:T(8,128)} %convolution_add_fusion.1), kind=kOutput, calls=%fused_computation.99 | convolution fusion | flops 5695488000 | bytes 26025984 | tf_op jit(solution)/shard_map/rf,rd->fd/dot_general | solution.py:269
  445.8 13.0 %fusion.38 = f32[768,3072]{1,0:T(8,128)} fusion(bf16[1200,3072]{1,0:T(8,128)(2,1)} %get-tuple-element.199, f32[1200,768]{1,0:T(8,128)} %copy-done.5, f32[768]{0:T(1024)S(1)} %copy-done.38, f32[768]{0:T(1024)S(1)} %copy-done.33, f32[1200]{0:T(1024)S(1)} %copy-done.27, f32[1200]{0:T(1024)S(1)} %copy-done.14), kind=kOutput, calls=%fused_computation.98 | convolution fusion | flops 5666918400 | bytes 20512128 | tf_op jit(solution)/shard_map/rd,rf->df/dot_general | solution.py:273
  460.9 8.9 %copy.56 = bf16[2,600,2304]{2,1,0:T(8,128)(2,1)} copy(bf16[2,600,2304]{1,2,0:T(8,128)(2,1)} %get-tuple-element.86) | data formatting | bytes 11059200 | tf_op jit(solution)/shard_map/while | solution.py:285
  469.8 3.8 convert_reduce_fusion.1
  474.2 10.7 %fusion.40 = (f32[768]{0:T(1024)S(1)}, f32[768]{0:T(1024)S(1)}, f32[1200]{0:T(1024)S(1)}, f32[1200]{0:T(1024)S(1)}, f32[1200,768]{1,0:T(8,128)}) fusion(f32[1200]{0:T(1024)S(1)} %copy-done.21, f32[1200]{0:T(1024)S(1)} %copy-done.16, bf16[2,600,768]{2,1,0:T(8,128)(2,1)S(1)} %copy-done.2, f32[1200,768]{1,0:T(8,128)S(1)} %copy-done.9, ...), kind=kOutput, calls=%fused_computation.100 | convolution fusion | flops 4255944704 | bytes 18312960 | tf_op jit(solution)/shard_map/re,de->rd/dot_general | solution.py:299
  484.9 42.3 %all-reduce.16 = (f32[768]{0:T(1024)S(1)}, f32[768]{0:T(1024)S(1)}, f32[1536]{0:T(1024)S(1)}, f32[768]{0:T(1024)S(1)}, f32[768]{0:T(1024)S(1)}, /*index=5*/f32[7...) all-reduce(f32[768]{0:T(1024)S(1)} %get-tuple-element.133, ...), channel_id=2, replica_groups=mesh['wide'=8,'narrow'=4] {'wide','narrow'}, use_global_device_ids=true, to_apply=%region_16.17.clone | all-reduce | flops 9216 | bytes 73728
  532.0 5.2 multiply_add_fusion
  537.2 14.2 %fusion.28 = bf16[1200,768]{1,0:T(8,128)(2,1)} fusion(f32[1200,768]{1,0:T(8,128)S(1)} %copy-done.7, bf16[3072,768]{1,0:T(8,128)(2,1)} %all-gather.11.cloned.1.call-done, f32[1200]{0:T(1024)S(1)} %copy-done.19, f32[768]{0:T(1024)S(1)} %convert_element_type.153, f32[1200,3072]{1,0:T(8,128)} %convolution_add_fusion.1), kind=kOutput, calls=%fused_computation.75 | convolution fusion | flops 5699174400 | bytes 25001664 | tf_op jit(solution)/shard_map/dot_general | solution.py:241
  551.4 139.3 %reduce-scatter.11.cloned.1.call-done = f32[96,768]{1,0:T(8,128)} async-done(((f32[3072,768]{1,0:T(8,128)}), f32[96,768]{1,0:T(8,128)}) %reduce-scatter.11.cloned.1.call-update) | async-done | bytes 294928 | tf_op jit(solution)/shard_map/reduce_scatter | solution.py:157
  690.7 142.1 %reduce-scatter.9.cloned.1.call-done = f32[24,3072]{1,0:T(8,128)} async-done(((f32[768,3072]{1,0:T(8,128)}), f32[24,3072]{1,0:T(8,128)}) %reduce-scatter.9.cloned.1.call-update) | async-done | bytes 294928 | tf_op jit(solution)/shard_map/reduce_scatter | solution.py:155
  (223 shorter events, 50.8 us)
Async XLA Ops:
  7.2 7.2 copy-start.45
  7.2 7.4 copy-start.49
  7.2 7.7 copy-start.50
  7.2 7.9 copy-start.51
  7.2 8.1 copy-start.52
  7.2 8.3 copy-start.53
  7.2 8.6 %copy-start.54 = (bf16[24]{0:T(256)(128)(2,1)S(1)}, bf16[24]{0:T(256)(128)(2,1)}, u32[]{:S(2)}) copy-start(bf16[24]{0:T(256)(128)(2,1)} %param.29) | copy-start | bytes 148
  7.3 8.8 %copy-start.55 = (bf16[48]{0:T(256)(128)(2,1)S(1)}, bf16[48]{0:T(256)(128)(2,1)}, u32[]{:S(2)}) copy-start(bf16[48]{0:T(256)(128)(2,1)} %param.26) | copy-start | bytes 292
  7.3 9.0 %copy-start.56 = (bf16[96]{0:T(256)(128)(2,1)S(1)}, bf16[96]{0:T(256)(128)(2,1)}, u32[]{:S(2)}) copy-start(bf16[96]{0:T(256)(128)(2,1)} %param.32) | copy-start | bytes 580
  7.3 66.6 %all-gather.5.cloned.1.call-start = ((), (), s32[]{:S(2)}) async-start(), calls=%async_computation.4 | async-start | bytes 3649536 | tf_op jit(solution)/shard_map/all_gather | solution.py:117
  8.0 163.0 %all-gather.7.cloned.1.call-start = ((), (), s32[]{:S(2)}) async-start(), calls=%async_computation.5 | async-start | bytes 1216512 | tf_op jit(solution)/shard_map/all_gather | solution.py:119
  8.8 186.4 %all-gather.9.cloned.1.call-start = ((), (), s32[]{:S(2)}) async-start(), calls=%async_computation.6 | async-start | bytes 4866048 | tf_op jit(solution)/shard_map/all_gather | solution.py:123
  9.5 250.9 %all-gather.11.cloned.1.call-start = ((), (), s32[]{:S(2)}) async-start(), calls=%async_computation.7 | async-start | bytes 4866048 | tf_op jit(solution)/shard_map/all_gather | solution.py:125
  10.1 541.4 %reduce-scatter.7.cloned.1.call-start = ((), (), s32[]{:S(2)}) async-start(), calls=%async_computation.9 | async-start | bytes 2433024 | tf_op jit(solution)/shard_map/reduce_scatter | solution.py:151
  10.1 54.8 %copy-start = (bf16[2,600,768]{2,1,0:T(8,128)(2,1)S(1)}, bf16[2,600,768]{2,1,0:T(8,128)(2,1)}, u32[]{:S(2)}) copy-start(bf16[2,600,768]{2,1,0:T(8,128)(2,1)} %param.20) | copy-start | bytes 5529604
  14.4 52.9 %copy-start.15 = (f32[1200]{0:T(1024)}, f32[1200]{0:T(1024)S(1)}, u32[]{:S(2)}) copy-start(f32[1200]{0:T(1024)S(1)} %div.35) | copy-start | bytes 14404
  14.5 46.5 %copy-start.22 = (f32[2,600]{1,0:T(2,128)}, f32[2,600]{1,0:T(2,128)S(1)}, u32[]{:S(2)}) copy-start(f32[2,600]{1,0:T(2,128)S(1)} %compare_convert_fusion) | copy-start | bytes 14404
  14.6 52.7 %copy-start.17 = (f32[1200]{0:T(1024)}, f32[1200]{0:T(1024)S(1)}, u32[]{:S(2)}) copy-start(f32[1200]{0:T(1024)S(1)} %reshape.369) | copy-start | bytes 14404
  14.6 52.7 %copy-start.28 = (f32[2,600]{1,0:T(2,128)}, f32[2,600]{1,0:T(2,128)S(1)}, u32[]{:S(2)}) copy-start(f32[2,600]{1,0:T(2,128)S(1)} %add_rsqrt_fusion.1) | copy-start | bytes 14404
  59.2 14.7 %copy-start.30 = (f32[768]{0:T(1024)}, f32[768]{0:T(1024)S(1)}, u32[]{:S(2)}) copy-start(f32[768]{0:T(1024)S(1)} %convert_element_type.142) | copy-start | bytes 9220
  59.8 14.1 %copy-start.39 = (f32[768]{0:T(1024)}, f32[768]{0:T(1024)S(1)}, u32[]{:S(2)}) copy-start(f32[768]{0:T(1024)S(1)} %convert_element_type.143) | copy-start | bytes 9220
  61.1 6.1 copy-start.20
  83.9 8.8 %copy-start.12 = (s32[2,600]{1,0:T(2,128)S(1)}, s32[2,600]{1,0:T(2,128)}, u32[]{:S(2)}) copy-start(s32[2,600]{1,0:T(2,128)} %param.22) | copy-start | bytes 14404
  92.7 78.3 %copy-start.1 = (bf16[2,600,768]{2,1,0:T(8,128)(2,1)S(1)}, bf16[2,600,768]{2,1,0:T(8,128)(2,1)}, u32[]{:S(2)}) copy-start(bf16[2,600,768]{2,1,0:T(8,128)(2,1)} %param.20) | copy-start | bytes 5529604
  92.7 78.3 %copy-start.41 = (f32[768]{0:T(1024)S(1)}, f32[768]{0:T(1024)}, u32[]{:S(2)}) copy-start(f32[768]{0:T(1024)} %convert_element_type.147) | copy-start | bytes 9220
  174.7 20.4 %copy-start.32 = (f32[768]{0:T(1024)S(1)}, f32[768]{0:T(1024)}, u32[]{:S(2)}) copy-start(f32[768]{0:T(1024)} %convert_element_type.148) | copy-start | bytes 9220
  174.7 20.4 %copy-start.35 = (f32[3072]{0:T(1024)S(1)}, f32[3072]{0:T(1024)}, u32[]{:S(2)}) copy-start(f32[3072]{0:T(1024)} %convert_element_type.151) | copy-start | bytes 36868
  174.7 20.4 %copy-start.37 = (f32[768]{0:T(1024)S(1)}, f32[768]{0:T(1024)}, u32[]{:S(2)}) copy-start(f32[768]{0:T(1024)} %convert_element_type.149) | copy-start | bytes 9220
  174.8 114.9 %copy-start.13 = (f32[1200]{0:T(1024)}, f32[1200]{0:T(1024)S(1)}, u32[]{:S(2)}) copy-start(f32[1200]{0:T(1024)S(1)} %broadcast_multiply_fusion.4) | copy-start | bytes 14404
  177.2 112.5 %copy-start.26 = (f32[1200]{0:T(1024)}, f32[1200]{0:T(1024)S(1)}, u32[]{:S(2)}) copy-start(f32[1200]{0:T(1024)S(1)} %add_rsqrt_fusion) | copy-start | bytes 14404
  177.2 83.2 %copy-start.10 = (bf16[1200,768]{1,0:T(8,128)(2,1)S(1)}, bf16[1200,768]{1,0:T(8,128)(2,1)}, u32[]{:S(2)}) copy-start(bf16[1200,768]{1,0:T(8,128)(2,1)} %fusion.27) | copy-start | bytes 5529604
  260.4 18.6 %copy-start.6 = (f32[1200,768]{1,0:T(8,128)S(1)}, f32[1200,768]{1,0:T(8,128)}, u32[]{:S(2)}) copy-start(f32[1200,768]{1,0:T(8,128)} %copy-done.5) | copy-start | bytes 11059204
  260.4 18.6 %copy-start.46 = (bf16[768,3072]{1,0:T(8,128)(2,1)S(1)}, bf16[768,3072]{1,0:T(8,128)(2,1)}, u32[]{:S(2)}) copy-start(bf16[768,3072]{1,0:T(8,128)(2,1)} %all-gather.9.cloned.1.call-done) | copy-start | bytes 14155780
  279.1 10.6 %copy-start.3 = (bf16[2,600,768]{2,1,0:T(8,128)(2,1)S(1)}, bf16[2,600,768]{2,1,0:T(8,128)(2,1)}, u32[]{:S(2)}) copy-start(bf16[2,600,768]{2,1,0:T(8,128)(2,1)} %param.35) | copy-start | bytes 5529604
  279.1 10.6 %copy-start.18 = (f32[1200]{0:T(1024)S(1)}, f32[1200]{0:T(1024)}, u32[]{:S(2)}) copy-start(f32[1200]{0:T(1024)} %copy-done.17) | copy-start | bytes 14404
  297.2 254.3 %reduce-scatter.5.cloned.1.call-start = ((), (), s32[]{:S(2)}) async-start(), calls=%async_computation.8 | async-start | bytes 7299072 | tf_op jit(solution)/shard_map/reduce_scatter | solution.py:149
  302.2 116.2 %copy-start.25 = (f32[2,600]{1,0:T(2,128)S(1)}, f32[2,600]{1,0:T(2,128)}, u32[]{:S(2)}) copy-start(f32[2,600]{1,0:T(2,128)} %copy-done.24) | copy-start | bytes 14404
  302.2 116.2 %copy-start.29 = (f32[2,600]{1,0:T(2,128)S(1)}, f32[2,600]{1,0:T(2,128)}, u32[]{:S(2)}) copy-start(f32[2,600]{1,0:T(2,128)} %copy-done.28) | copy-start | bytes 14404
  302.2 116.2 %copy-start.31 = (f32[768]{0:T(1024)S(1)}, f32[768]{0:T(1024)}, u32[]{:S(2)}) copy-start(f32[768]{0:T(1024)} %copy-done.30) | copy-start | bytes 9220
  302.2 116.2 %copy-start.40 = (f32[768]{0:T(1024)S(1)}, f32[768]{0:T(1024)}, u32[]{:S(2)}) copy-start(f32[768]{0:T(1024)} %copy-done.39) | copy-start | bytes 9220
  430.1 260.7 %reduce-scatter.11.cloned.1.call-start = ((), (), s32[]{:S(2)}) async-start(), calls=%async_computation.11 | async-start | bytes 9732096 | tf_op jit(solution)/shard_map/reduce_scatter | solution.py:157
  445.1 387.7 %reduce-scatter.9.cloned.1.call-start = ((), (), s32[]{:S(2)}) async-start(), calls=%async_computation.10 | async-start | bytes 9732096 | tf_op jit(solution)/shard_map/reduce_scatter | solution.py:155
  474.2 10.7 %copy-start.34 = (f32[768]{0:T(1024)S(1)}, f32[768]{0:T(1024)}, u32[]{:S(2)}) copy-start(f32[768]{0:T(1024)} %get-tuple-element.178) | copy-start | bytes 9220
  474.2 10.7 %copy-start.36 = (f32[3072]{0:T(1024)S(1)}, f32[3072]{0:T(1024)}, u32[]{:S(2)}) copy-start(f32[3072]{0:T(1024)} %get-tuple-element.198) | copy-start | bytes 36868
  474.2 10.7 %copy-start.42 = (f32[768]{0:T(1024)S(1)}, f32[768]{0:T(1024)}, u32[]{:S(2)}) copy-start(f32[768]{0:T(1024)} %get-tuple-element.126) | copy-start | bytes 9220
  474.2 10.7 %copy-start.43 = (f32[768]{0:T(1024)S(1)}, f32[768]{0:T(1024)}, u32[]{:S(2)}) copy-start(f32[768]{0:T(1024)} %get-tuple-element.131) | copy-start | bytes 9220
  532.0 5.2 copy-start.7
  532.0 5.2 copy-start.19
  (17 other events, 38.7 us)
Sparse Core Ops, SparseCore 0:
  11.0 62.8 all-gather.4
  76.8 52.8 all-gather.6
  132.6 62.5 all-gather.8
  197.9 62.4 all-gather.10
  297.3 97.8 reduce-scatter.6
  430.2 119.0 reduce-scatter.4
  555.8 134.9 reduce-scatter.10
  698.2 134.5 reduce-scatter.8
where the time goes:
time: 848 us; the launch traced here: 840 us
  waiting for transfers between devices  361 us (43%)
  matrix products  243 us (29%)
  blocking collectives  85.1 us (10%)
  other arithmetic  78.9 us (9%)
  local copies, waits for them, and re-layouts  55.3 us (7%)
  between operations  14.9 us (2%)
    reduce_scatter x1, waiting for transfers between devices, reduce_grads(): lax.psum_scatter(w_up, ('wide', 'narrow'), scatter_dimension=0, tiled=True)  142 us
    reduce_scatter x1, waiting for transfers between devices, reduce_grads(): lax.psum_scatter(w_down, ('wide', 'narrow'), scatter_dimension=0, tiled=T...  139 us
    unnamed x2, blocking collectives  85.1 us
    all_gather x1, waiting for transfers between devices, fetch(): lax.all_gather(w_down, ('wide', 'narrow'), axis=0, tiled=True)  52.9 us
    dot_general x4, matrix products, score_table(): jnp.einsum('qhd,khd->hqk', queries, key_rows, preferred_element_type=jnp....  32.6 us
    convert_element_type x2, other arithmetic, attend_backward(): (probs * (d_probs - jnp.sum(probs * d_probs, axis=-1, keepdims=True))).as...  26.5 us
    dot_general x2, matrix products, attend_backward(): jnp.einsum('qhd,khd->hqk', d_heads, value_rows, preferred_element_type=jn...  26.3 us
    dot_general x2, matrix products, attend_forward(): jnp.einsum('hqk,khd->qhd', probs_low, head_split(qkv_item, 2), preferred_...  26 us
  transfers between devices with their start and end apart: 8, of which 5 were waited for; matrix products, arithmetic and copies ran while one was open for 40% of the time, Pallas kernels for 0%

commit v1 on v0

--- a/solution.py
+++ b/solution.py
@@ -1,3 +1,4 @@
+import functools
 from functools import partial
 import jax
 import jax.numpy as jnp
@@ -9,6 +10,35 @@
 HEAD = 64
 norm_epsilon = 1e-05
 masked_score = -1e30
+
+
+def move_boxes(mine, dim_i):
+    mine = jnp.moveaxis(mine, 0, dim_i)
+    a_next = mine.shape
+    odd = mine.reshape(*a_next[:dim_i], a_next[dim_i] * a_next[dim_i + 1], *a_next[dim_i + 2 :])
+    return odd
+
+
+def _wrap_counts(m, named_axis):
+    u_next = m[None]
+    amount_of = lax.psum(1, axis_name=named_axis)
+    for idx in range(amount_of.bit_length() - 1):
+        y_new = 1 << idx
+        block_now = lax.ppermute(
+            u_next, axis_name=named_axis, perm=tuple(((u, u ^ y_new) for u in range(amount_of)))
+        )
+        k_now = jnp.stack([u_next, block_now], axis=0)
+        current_value = lax.axis_index(named_axis) >> idx & 1
+        u_next = jnp.where(current_value == 0, k_now, k_now[::-1]).reshape(-1, *m.shape)
+    return u_next
+
+
+def _measure_loads(xin, q_in, array_axis):
+    lower = move_boxes(_wrap_counts(xin, q_in), array_axis)
+    return lower
+
+
+test_thing = functools.partial(_measure_loads, q_in=("wide", "narrow"), array_axis=0)
 
 
 def layer_norm(values, gain, shift):
@@ -122,7 +152,7 @@
         lax.all_gather(shift_two, ("wide", "narrow"), axis=0, tiled=True),
         lax.all_gather(w_up, ("wide", "narrow"), axis=0, tiled=True),
         lax.all_gather(bias_up, ("wide", "narrow"), axis=0, tiled=True),
-        lax.all_gather(w_down, ("wide", "narrow"), axis=0, tiled=True),
+        test_thing(w_down),
         lax.all_gather(bias_down, ("wide", "narrow"), axis=0, tiled=True),
     )
     return whole_set

time: 848 us -> 929 us (1.096)
  blocking collectives: 85.1 us -> 165 us
  waiting for transfers between devices: 361 us -> 346 us
  other arithmetic: 78.9 us -> 88.4 us
    unnamed x2, blocking collectives: 85.1 us -> 165 us
    ppermute x0 -> x5, waiting for transfers between devices: none -> 61.6 us  [_wrap_counts(): lax.ppermute(u_next, axis_name=named_axis, perm=tuple(((u, u ^ y_new) for...]
    all_gather x1 -> x0, waiting for transfers between devices: 52.9 us -> none  [fetch(): lax.all_gather(w_down, ('wide', 'narrow'), axis=0, tiled=True)]
    all_gather x1, waiting for transfers between devices: 18 us -> 0.02 us  [fetch(): lax.all_gather(w_up, ('wide', 'narrow'), axis=0, tiled=True)]
  transfers between devices with their start and end apart: 8 -> 12, of which waited for: 5 -> 7; matrix products, arithmetic and copies ran while one was open for 40% -> 36% of each run, Pallas kernels for 0% -> 0%
where the time goes in v1:
time: 929 us; the launch traced here: 924 us
  waiting for transfers between devices  346 us (37%)
  matrix products  243 us (26%)
  blocking collectives  165 us (18%)
  other arithmetic  88.4 us (10%)
  local copies, waits for them, and re-layouts  56 us (6%)
  between operations  14.9 us (2%)
  starting transfers between devices  9.47 us (1%)
    unnamed x2, blocking collectives  165 us
    reduce_scatter x1, waiting for transfers between devices, reduce_grads(): lax.psum_scatter(w_up, ('wide', 'narrow'), scatter_dimension=0, tiled=True)  142 us
    reduce_scatter x1, waiting for transfers between devices, reduce_grads(): lax.psum_scatter(w_down, ('wide', 'narrow'), scatter_dimension=0, tiled=T...  141 us
    ppermute x5, waiting for transfers between devices, _wrap_counts(): lax.ppermute(u_next, axis_name=named_axis, perm=tuple(((u, u ^ y_new) for...  61.6 us
    dot_general x4, matrix products, score_table(): jnp.einsum('qhd,khd->hqk', queries, key_rows, preferred_element_type=jnp....  32.7 us
    convert_element_type x2, other arithmetic, attend_backward(): (probs * (d_probs - jnp.sum(probs * d_probs, axis=-1, keepdims=True))).as...  26.5 us
    dot_general x2, matrix products, attend_backward(): jnp.einsum('qhd,khd->hqk', d_heads, value_rows, preferred_element_type=jn...  26.3 us
    dot_general x2, matrix products, attend_forward(): jnp.einsum('hqk,khd->qhd', probs_low, head_split(qkv_item, 2), preferred_...  26.1 us
  transfers between devices with their start and end apart: 12, of which 7 were waited for; matrix products, arithmetic and copies ran while one was open for 36% of the time, Pallas kernels for 0%

profile of v1, /device:TPU:0, one launch (start us, length us, event | category | flops | bytes accessed | tf_op | source)
XLA Modules:
  0.0 923.9 jit_solution(2114445409657151508)
XLA Ops:
  10.7 2.9 collective-permute-start.1
  13.7 7.2 collective-permute-done.1
  22.9 13.9 %collective-permute-done.2 = bf16[4,96,768]{2,1,0:T(8,128)(2,1)S(1)} collective-permute-done((bf16[4,96,768]{2,1,0:T(8,128)(2,1)S(1)}, bf16[4,96,768]{2,1,0:T(8,128)(2,1)S(1)}, u32[]{:S(2)}, u32[]{:S(2)}) %collective-permute-start.2) | collective-permute-done | bytes 589856 | tf_op jit(solution)/shard_map/ppermute | solution.py:27
  38.8 39.2 %collective-permute-done.3 = bf16[8,96,768]{2,1,0:T(8,128)(2,1)S(1)} collective-permute-done((bf16[8,96,768]{2,1,0:T(8,128)(2,1)S(1)}, bf16[8,96,768]{2,1,0:T(8,128)(2,1)S(1)}, u32[]{:S(2)}, u32[]{:S(2)}) %collective-permute-start.3) | collective-permute-done | bytes 1179680 | tf_op jit(solution)/shard_map/ppermute | solution.py:27
  82.7 2.3 collective-permute-start.4
  87.4 123.6 %all-reduce.17 = (bf16[1536]{0:T(1024)(128)(2,1)S(1)}, bf16[768]{0:T(1024)(128)(2,1)S(1)}, bf16[768]{0:T(1024)(128)(2,1)S(1)}, bf16[768]{0:T(1024)(128)(2,1)S(1)...) all-reduce(bf16[1536]{0:T(1024)(128)(2,1)S(1)} %dynamic-update-slic, ...), channel_id=1, replica_groups=mesh['wide'=8,'narrow'=4] {'wide','narrow'}, use_global_device_ids=true, to_apply=%add.2 | all-reduce | flops 9216 | bytes 36864
  215.0 3.9 convert_reduce_fusion.2
  219.0 2.4 fusion.26
  221.4 2.8 pad_maximum_fusion
  224.2 3.2 reverse_select_fusion
  227.4 10.0 %fusion.22 = bf16[1200,2304]{1,0:T(8,128)(2,1)} fusion(bf16[768,2304]{1,0:T(8,128)(2,1)} %all-gather.4.cloned.1.call-done, f32[2304]{0:T(1024)S(1)} %pad_maximum_fusion.5, f32[1200,768]{1,0:T(8,128)} %fusion.26, f32[768]{0:T(1024)S(1)} %convert_element_type.147, f32[768]{0:T(1024)S(1)} %convert_element_type.146), kind=kOutput, calls=%fused_computation.47 | convolution fusion | flops 4255027200 | bytes 12770304 | tf_op jit(solution)/shard_map/dot_general | solution.py:251
  237.5 8.8 copy.52
  246.3 78.5 %while.22 = (s32[]{:T(128)}, bf16[2,600,768]{2,1,0:T(8,128)(2,1)}, f32[2,12,600,1]{2,1,3,0:T(8,128)S(1)}, bf16[2,600,2304]{1,2,0:T(8,128)(2,1)}, s32[2,600]{1,0:T(2,128)S(1)}, /*index=5*/s32[2]{0:T(128)S(1)}, s32[]{:T(128)}) while((s32[]{:T(128)}, bf16[2,600,768]{2,1,0:T(8,128)(2,1)}, f32[2,12,600,1]{2,1,3,0:T(8,128)S(1)}, ...), condition=%wide.region_5.6_spmd, body=%wide.region_2.5_spmd.sunk | while | flops 1158934144 | bytes 71987392 | solution.py:255
  251.4 8.2 fusion.101
  259.6 10.3 %fusion.102 = f32[12,600]{1,0:T(8,128)S(1)} fusion(f32[12,600,600]{1,2,0:T(8,128)} %get-tuple-element.293, f32[12,600]{1,0:T(8,128)S(1)} %get-tuple-element.294, pred[600,600]{0,1:T(8,128)(4,1)S(1)} %compare_and_fusion.4), kind=kLoop, calls=%fused_computation.4.clone.1 | loop fusion | flops 17272800 | bytes 17697600 | tf_op jit(solution)/shard_map/while/body/eval_jaxpr/reduce_sum | solution.py:86
  269.9 13.1 %fusion.103 = bf16[12,64,600]{2,1,0:T(8,128)(2,1)} fusion(bf16[600,12,64]{0,2,1:T(8,128)(2,1)} %bitcast.171, f32[12,600,600]{1,2,0:T(8,128)} %get-tuple-element.293, f32[12,600]{1,0:T(8,128)S(1)} %fusion.102, f32[12,600]{1,0:T(8,128)S(1)} %get-tuple-element.294, pred[600,600]{0,1:T(8,128)(4,1)S(1)} %compare_and_fusion.4), kind=kOutput, calls=%fused_computation.8.clone.1 | convolution fusion | flops 575020800 | bytes 19540800 | tf_op jit(solution)/shard_map/while/body/eval_jaxpr/hqk,khd->qhd/dot_general | solution.py:88
  290.5 8.2 fusion.101
  298.7 10.1 %fusion.102 = f32[12,600]{1,0:T(8,128)S(1)} fusion(f32[12,600,600]{1,2,0:T(8,128)} %get-tuple-element.293, f32[12,600]{1,0:T(8,128)S(1)} %get-tuple-element.294, pred[600,600]{0,1:T(8,128)(4,1)S(1)} %compare_and_fusion.4), kind=kLoop, calls=%fused_computation.4.clone.1 | loop fusion | flops 17272800 | bytes 17697600 | tf_op jit(solution)/shard_map/while/body/eval_jaxpr/reduce_sum | solution.py:86
  308.8 13.0 %fusion.103 = bf16[12,64,600]{2,1,0:T(8,128)(2,1)} fusion(bf16[600,12,64]{0,2,1:T(8,128)(2,1)} %bitcast.171, f32[12,600,600]{1,2,0:T(8,128)} %get-tuple-element.293, f32[12,600]{1,0:T(8,128)S(1)} %fusion.102, f32[12,600]{1,0:T(8,128)S(1)} %get-tuple-element.294, pred[600,600]{0,1:T(8,128)(4,1)S(1)} %compare_and_fusion.4), kind=kOutput, calls=%fused_computation.8.clone.1 | convolution fusion | flops 575020800 | bytes 19540800 | tf_op jit(solution)/shard_map/while/body/eval_jaxpr/hqk,khd->qhd/dot_general | solution.py:88
  324.9 3.7 fusion.47
  331.0 12.5 %convolution_add_fusion.1 = f32[1200,3072]{1,0:T(8,128)} fusion(bf16[768,3072]{1,0:T(8,128)(2,1)} %all-gather.8.cloned.1.call-done, f32[3072]{0:T(1024)S(1)} %copy-done.33, f32[1200,768]{1,0:T(8,128)} %copy-done.3, f32[768]{0:T(1024)S(1)} %copy-done.35, f32[768]{0:T(1024)S(1)} %copy-done.29, f32[1200]{0:T(1024)S(1)} %add_rsqrt_fusion, ...), kind=kOutput, calls=%fused_computation.45 | convolution fusion | flops 5670604800 | bytes 23178624 | tf_op jit(solution)/shard_map/dot_general | solution.py:266
  343.5 18.6 %convert_reduce_fusion = (f32[3072]{0:T(1024)}, bf16[1200,3072]{1,0:T(8,128)(2,1)}) fusion(f32[1200,3072]{1,0:T(8,128)} %convolution_add_fusion.1, bf16[1200,768]{1,0:T(8,128)(2,1)S(1)} %bitcast.183, bf16[3072,768]{1,0:T(8,128)(2,1)} %bitcast.176), kind=kOutput, calls=%fused_computation.42 | convolution fusion | flops 5743408128 | bytes 28692480 | tf_op jit(solution)/shard_map/rd,fd->rf/dot_general | solution.py:300
  362.2 10.6 %multiply_reduce_fusion.1 = (f32[768]{0:T(1024)}, f32[1200]{0:T(1024)S(1)}, f32[1200]{0:T(1024)S(1)}, f32[768]{0:T(1024)}, f32[1200,768]{1,0:T(8,128)S(1)}) fusion(f32[1200,768]{1,0:T(8,128)S(1)} %copy-done.4, f32[1200]{0:T(1024)S(1)} %add_rsqrt_fusion, f32[1200]{0:T(1024)S(1)} %broadcast_multiply_fusion.4, f32[768]{0:T(1024)S(1)} %copy-done.29, ...), kind=kOutput, calls=%fused_computation.60 | convolution fusion | flops 5670600704 | bytes 19492608 | tf_op jit(solution)/shard_map/rf,df->rd/dot_general | solution.py:304
  372.9 3.3 convert_reduce_fusion.3
  378.1 3.2 fusion.37
  381.4 4.9 convolution_convert_fusion
  386.3 116.0 %while.23 = (s32[]{:T(128)}, bf16[2,600,2304]{1,2,0:T(8,128)(2,1)}, bf16[2,600,2304]{1,2,0:T(8,128)(2,1)}, s32[2,600]{1,0:T(2,128)S(1)}, s32[2]{0:T(128)S(1)}, /...) while((s32[]{:T(128)}, bf16[2,600,2304]{1,2,0:T(8,128)(2,1)}, ...), condition=%wide.region_12.13_spmd, body=%wide.region_10.12_spmd.sunk | while | flops 2840911872 | bytes 160925648 | solution.py:315
  392.5 8.2 fusion.115
  400.6 11.0 %fusion.116 = bf16[12,64,600]{2,1,0:T(8,128)(2,1)S(1)} fusion(bf16[600,12,64]{0,2,1:T(8,128)(2,1)S(1)} %bitcast.167, f32[12,600,600]{1,2,0:T(8,128)} %fusion.115, f32[12,600]{1,0:T(8,128)S(1)} %dynamic-slice_bitcast_fusion.8, pred[600,600]{0,1:T(8,128)(4,1)S(1)} %compare_and_fusion.5), kind=kOutput, calls=%fused_computation.26.clone.1 | convolution fusion | flops 570700800 | bytes 19512000 | tf_op jit(solution)/shard_map/while/body/eval_jaxpr/hqk,qhd->khd/dot_general | solution.py:107
  411.7 13.2 %multiply_reduce_fusion.10 = (f32[12,600]{1,0:T(8,128)S(1)}, f32[12,600,600]{1,2,0:T(8,128)}) fusion(f32[12,600,600]{1,2,0:T(8,128)} %fusion.115, f32[12,600]{1,0:T(8,128)S(1)} %dynamic-slice_bitcast_fusion.8, pred[600,600]{0,1:T(8,128)(4,1)S(1)} %compare_and_fusion.5, bf16[600,12,64]{0,2,1:T(8,128)(2,1)S(1)} %bitcast.168, ...), kind=kOutput, calls=%fused_computation.16.clone.1 | convolution fusion | flops 574552832 | bytes 36820800 | tf_op jit(solution)/shard_map/while/body/eval_jaxpr/qhd,khd->hqk/dot_general | solution.py:108
  424.9 13.4 %multiply_convert_fusion.11 = bf16[12,600,600]{1,2,0:T(8,128)(2,1)S(1)} fusion(f32[12,600,600]{1,2,0:T(8,128)} %get-tuple-element.305, f32[12,600,600]{1,2,0:T(8,128)} %fusion.115, f32[12,600]{1,0:T(8,128)S(1)} %get-tuple-element.306, f32[12,600]{1,0:T(8,128)S(1)} %dynamic-slice_bitcast_fusion.8, pred[600,600]{0,1:T(8,128)(4,1)S(1)} %compare_and_fusion.5), kind=kLoop, calls=%fused_computation.15.clone.1 | loop fusion | flops 25920000 | bytes 43617600 | tf_op jit(solution)/shard_map/while/body/eval_jaxpr/convert_element_type | solution.py:109
  440.0 2.8 multiply_convert_fusion.12
  450.6 8.1 fusion.115
  458.7 10.8 %fusion.116 = bf16[12,64,600]{2,1,0:T(8,128)(2,1)S(1)} fusion(bf16[600,12,64]{0,2,1:T(8,128)(2,1)S(1)} %bitcast.167, f32[12,600,600]{1,2,0:T(8,128)} %fusion.115, f32[12,600]{1,0:T(8,128)S(1)} %dynamic-slice_bitcast_fusion.8, pred[600,600]{0,1:T(8,128)(4,1)S(1)} %compare_and_fusion.5), kind=kOutput, calls=%fused_computation.26.clone.1 | convolution fusion | flops 570700800 | bytes 19512000 | tf_op jit(solution)/shard_map/while/body/eval_jaxpr/hqk,qhd->khd/dot_general | solution.py:107
  469.5 13.1 %multiply_reduce_fusion.10 = (f32[12,600]{1,0:T(8,128)S(1)}, f32[12,600,600]{1,2,0:T(8,128)}) fusion(f32[12,600,600]{1,2,0:T(8,128)} %fusion.115, f32[12,600]{1,0:T(8,128)S(1)} %dynamic-slice_bitcast_fusion.8, pred[600,600]{0,1:T(8,128)(4,1)S(1)} %compare_and_fusion.5, bf16[600,12,64]{0,2,1:T(8,128)(2,1)S(1)} %bitcast.168, ...), kind=kOutput, calls=%fused_computation.16.clone.1 | convolution fusion | flops 574552832 | bytes 36820800 | tf_op jit(solution)/shard_map/while/body/eval_jaxpr/qhd,khd->hqk/dot_general | solution.py:108
  482.7 13.0 %multiply_convert_fusion.11 = bf16[12,600,600]{1,2,0:T(8,128)(2,1)S(1)} fusion(f32[12,600,600]{1,2,0:T(8,128)} %get-tuple-element.305, f32[12,600,600]{1,2,0:T(8,128)} %fusion.115, f32[12,600]{1,0:T(8,128)S(1)} %get-tuple-element.306, f32[12,600]{1,0:T(8,128)S(1)} %dynamic-slice_bitcast_fusion.8, pred[600,600]{0,1:T(8,128)(4,1)S(1)} %compare_and_fusion.5), kind=kLoop, calls=%fused_computation.15.clone.1 | loop fusion | flops 25920000 | bytes 43617600 | tf_op jit(solution)/shard_map/while/body/eval_jaxpr/convert_element_type | solution.py:109
  497.4 2.8 multiply_convert_fusion.12
  502.4 11.7 %convolution_bitcast_fusion = f32[768,2304]{1,0:T(8,128)} fusion(bf16[2,600,2304]{1,2,0:T(8,128)(2,1)} %get-tuple-element.86, bf16[2,600,768]{2,1,0:T(8,128)(2,1)} %param.20, f32[768]{0:T(1024)S(1)} %copy-done.38, f32[768]{0:T(1024)S(1)} %copy-done.28, f32[2,600]{1,0:T(2,128)S(1)} %copy-done.26, f32[2,600]{1,0:T(2,128)S(1)} %copy-done.20), kind=kOutput, calls=%fused_computation.49 | convolution fusion | flops 4252262400 | bytes 14466432 | tf_op jit(solution)/shard_map/rd,re->de/dot_general | solution.py:328
  515.5 13.5 %fusion.41 = f32[3072,768]{1,0:T(8,128)} fusion(bf16[1200,768]{1,0:T(8,128)(2,1)S(1)} %copy-done.9, f32[1200,3072]{1,0:T(8,128)} %convolution_add_fusion.1), kind=kOutput, calls=%fused_computation.111 | convolution fusion | flops 5695488000 | bytes 26025984 | tf_op jit(solution)/shard_map/rf,rd->fd/dot_general | solution.py:299
  529.8 13.2 %fusion.40 = f32[768,3072]{1,0:T(8,128)} fusion(bf16[1200,3072]{1,0:T(8,128)(2,1)} %get-tuple-element.204, f32[1200,768]{1,0:T(8,128)} %copy-done.3, f32[768]{0:T(1024)S(1)} %copy-done.36, f32[768]{0:T(1024)S(1)} %copy-done.30, f32[1200]{0:T(1024)S(1)} %copy-done.24, f32[1200]{0:T(1024)S(1)} %copy-done.14), kind=kOutput, calls=%fused_computation.110 | convolution fusion | flops 5666918400 | bytes 20512128 | tf_op jit(solution)/shard_map/rd,rf->df/dot_general | solution.py:303
  543.7 9.0 copy.56
  552.6 3.9 convert_reduce_fusion.1
  557.2 10.7 %fusion.42 = (f32[768]{0:T(1024)S(1)}, f32[768]{0:T(1024)S(1)}, f32[1200]{0:T(1024)S(1)}, f32[1200]{0:T(1024)S(1)}, f32[1200,768]{1,0:T(8,128)}) fusion(f32[1200]{0:T(1024)S(1)} %copy-done.18, f32[1200]{0:T(1024)S(1)} %copy-done.16, bf16[2,600,768]{2,1,0:T(8,128)(2,1)S(1)} %copy-done.2, f32[1200,768]{1,0:T(8,128)S(1)} %copy-done.8, ...), kind=kOutput, calls=%fused_computation.112 | convolution fusion | flops 4255944704 | bytes 18312960 | tf_op jit(solution)/shard_map/re,de->rd/dot_general | solution.py:329
  567.9 41.0 %all-reduce.16 = (f32[768]{0:T(1024)S(1)}, f32[768]{0:T(1024)S(1)}, f32[1536]{0:T(1024)S(1)}, f32[768]{0:T(1024)S(1)}, f32[768]{0:T(1024)S(1)}, /*index=5*/f32[7...) all-reduce(f32[768]{0:T(1024)S(1)} %get-tuple-element.133, ...), channel_id=2, replica_groups=mesh['wide'=8,'narrow'=4] {'wide','narrow'}, use_global_device_ids=true, to_apply=%region_16.17.clone | all-reduce | flops 9216 | bytes 73728
  613.6 5.2 multiply_add_fusion
  618.8 14.4 %fusion.28 = bf16[1200,768]{1,0:T(8,128)(2,1)} fusion(f32[1200,768]{1,0:T(8,128)S(1)} %copy-done.5, bf16[3072,768]{1,0:T(8,128)(2,1)} %bitcast.177, f32[1200]{0:T(1024)S(1)} %copy-done.22, f32[768]{0:T(1024)S(1)} %convert_element_type.157, f32[1200,3072]{1,0:T(8,128)} %convolution_add_fusion.1), kind=kOutput, calls=%fused_computation.78 | convolution fusion | flops 5699174400 | bytes 25001664 | tf_op jit(solution)/shard_map/dot_general | solution.py:271
  633.6 141.3 %reduce-scatter.11.cloned.1.call-done = f32[96,768]{1,0:T(8,128)} async-done(((f32[3072,768]{1,0:T(8,128)}), f32[96,768]{1,0:T(8,128)}) %reduce-scatter.11.cloned.1.call-update) | async-done | bytes 294928 | tf_op jit(solution)/shard_map/reduce_scatter | solution.py:187
  774.9 142.0 %reduce-scatter.9.cloned.1.call-done = f32[24,3072]{1,0:T(8,128)} async-done(((f32[768,3072]{1,0:T(8,128)}), f32[24,3072]{1,0:T(8,128)}) %reduce-scatter.9.cloned.1.call-update) | async-done | bytes 294928 | tf_op jit(solution)/shard_map/reduce_scatter | solution.py:185
  (238 shorter events, 65.1 us)
Async XLA Ops:
  7.2 220.3 %all-gather.4.cloned.1.call-start = ((), (), s32[]{:S(2)}) async-start(), calls=%async_computation.4 | async-start | bytes 3649536 | tf_op jit(solution)/shard_map/all_gather | solution.py:147
  7.9 316.9 %all-gather.6.cloned.1.call-start = ((), (), s32[]{:S(2)}) async-start(), calls=%async_computation.5 | async-start | bytes 1216512 | tf_op jit(solution)/shard_map/all_gather | solution.py:149
  8.0 1.7 collective-permute-start
  10.7 10.2 %collective-permute-start.1 = (bf16[2,96,768]{2,1,0:T(8,128)(2,1)S(1)}, bf16[2,96,768]{2,1,0:T(8,128)(2,1)S(1)}, u32[]{:S(2)}, u32[]{:S(2)}) collective-permute-start(bf16[2,96,768]{2,1,0:T(8,128)(2,1)S(1)} %get-tuple-element.194), channel_id=1, source_target_pairs={{0,2},{1,3},{2,0},{3,1},{4,6},{5,7},{6,4},{7,5},{8,10},{9,11},{10,... | collective-permute-start | bytes 884744 | tf_op jit(solution)/shard_map/ppermute | solution.py:27
  13.6 317.3 %all-gather.8.cloned.1.call-start = ((), (), s32[]{:S(2)}) async-start(), calls=%async_computation.6 | async-start | bytes 4866048 | tf_op jit(solution)/shard_map/all_gather | solution.py:153
  21.1 15.7 %collective-permute-start.2 = (bf16[4,96,768]{2,1,0:T(8,128)(2,1)S(1)}, bf16[4,96,768]{2,1,0:T(8,128)(2,1)S(1)}, u32[]{:S(2)}, u32[]{:S(2)}) collective-permute-start(bf16[4,96,768]{2,1,0:T(8,128)(2,1)S(1)} %bitcast.181), channel_id=1, source_target_pairs={{0,4},{1,5},{2,6},{3,7},{4,0},{5,1},{6,2},{7,3},{8,12},{9,13},{10,... | collective-permute-start | bytes 1769480 | tf_op jit(solution)/shard_map/ppermute | solution.py:27
  37.2 40.9 %collective-permute-start.3 = (bf16[8,96,768]{2,1,0:T(8,128)(2,1)S(1)}, bf16[8,96,768]{2,1,0:T(8,128)(2,1)S(1)}, u32[]{:S(2)}, u32[]{:S(2)}) collective-permute-start(bf16[8,96,768]{2,1,0:T(8,128)(2,1)S(1)} %bitcast.178), channel_id=1, source_target_pairs={{0,8},{1,9},{2,10},{3,11},{4,12},{5,13},{6,14},{7,15},{8,0},{9,1},... | collective-permute-start | bytes 3538952 | tf_op jit(solution)/shard_map/ppermute | solution.py:27
  38.8 594.4 %reduce-scatter.7.cloned.1.call-start = ((), (), s32[]{:S(2)}) async-start(), calls=%async_computation.8 | async-start | bytes 2433024 | tf_op jit(solution)/shard_map/reduce_scatter | solution.py:181
  79.1 6.0 copy-start
  80.7 5.2 copy-start.48
  80.7 5.4 copy-start.49
  80.7 5.6 copy-start.50
  80.7 5.9 copy-start.51
  80.8 6.1 copy-start.52
  80.8 6.3 copy-start.53
  80.8 132.9 %copy-start.43 = (s32[2]{0:T(128)S(1)}, s32[2]{0:T(128)}, u32[]{:S(2)}) copy-start(s32[2]{0:T(128)} %param.21) | copy-start | bytes 28
  82.7 138.7 %collective-permute-start.4 = (bf16[16,96,768]{2,1,0:T(8,128)(2,1)}, bf16[16,96,768]{2,1,0:T(8,128)(2,1)}, u32[]{:S(2)}, u32[]{:S(2)}) collective-permute-start(bf16[16,96,768]{2,1,0:T(8,128)(2,1)} %bitcast.37), channel_id=1, source_target_pairs={{0,16},{1,17},{2,18},{3,19},{4,20},{5,21},{6,22},{7,23},{8,24},{9,... | collective-permute-start | bytes 7077896 | tf_op jit(solution)/shard_map/ppermute | solution.py:27
  211.0 16.5 %copy-start.27 = (f32[768]{0:T(1024)}, f32[768]{0:T(1024)S(1)}, u32[]{:S(2)}) copy-start(f32[768]{0:T(1024)S(1)} %convert_element_type.146) | copy-start | bytes 9220
  211.6 15.9 %copy-start.37 = (f32[768]{0:T(1024)}, f32[768]{0:T(1024)S(1)}, u32[]{:S(2)}) copy-start(f32[768]{0:T(1024)S(1)} %convert_element_type.147) | copy-start | bytes 9220
  212.8 8.5 copy-start.15
  213.6 7.8 copy-start.25
  213.7 7.7 copy-start.17
  237.5 8.8 copy-start.12
  246.3 78.6 %copy-start.1 = (bf16[2,600,768]{2,1,0:T(8,128)(2,1)S(1)}, bf16[2,600,768]{2,1,0:T(8,128)(2,1)}, u32[]{:S(2)}) copy-start(bf16[2,600,768]{2,1,0:T(8,128)(2,1)} %param.20) | copy-start | bytes 5529604
  246.3 78.6 %copy-start.39 = (f32[768]{0:T(1024)S(1)}, f32[768]{0:T(1024)}, u32[]{:S(2)}) copy-start(f32[768]{0:T(1024)} %convert_element_type.151) | copy-start | bytes 9220
  328.6 44.2 %copy-start.13 = (f32[1200]{0:T(1024)}, f32[1200]{0:T(1024)S(1)}, u32[]{:S(2)}) copy-start(f32[1200]{0:T(1024)S(1)} %broadcast_multiply_fusion.4) | copy-start | bytes 14404
  330.9 41.9 %copy-start.23 = (f32[1200]{0:T(1024)}, f32[1200]{0:T(1024)S(1)}, u32[]{:S(2)}) copy-start(f32[1200]{0:T(1024)S(1)} %add_rsqrt_fusion) | copy-start | bytes 14404
  330.9 12.6 %copy-start.10 = (bf16[2,600,768]{2,1,0:T(8,128)(2,1)S(1)}, bf16[2,600,768]{2,1,0:T(8,128)(2,1)}, u32[]{:S(2)}) copy-start(bf16[2,600,768]{2,1,0:T(8,128)(2,1)} %get-tuple-element.179) | copy-start | bytes 5529604
  331.0 31.2 %slice-start = ((s8[4718592]{0:T(1024)(128)(4,1)}), s8[4194304]{0:T(1024)(128)(4,1)S(1)}, s32[]{:S(2)}) async-start(s8[4718592]{0:T(1024)(128)(4,1)} %bitcast.190), calls=%async_computation.11 | async-start | bytes 8388608
  343.5 18.7 %copy-start.4 = (f32[1200,768]{1,0:T(8,128)S(1)}, f32[1200,768]{1,0:T(8,128)}, u32[]{:S(2)}) copy-start(f32[1200,768]{1,0:T(8,128)} %copy-done.3) | copy-start | bytes 11059204
  343.5 18.7 %slice-start.1 = ((s8[4718592]{0:T(1024)(128)(4,1)}), s8[524288]{0:T(1024)(128)(4,1)S(1)}, s32[]{:S(2)}) async-start(s8[4718592]{0:T(1024)(128)(4,1)} %bitcast.190), calls=%async_computation.12 | async-start | bytes 1048576
  362.2 10.7 %copy-start.7 = (bf16[2,600,768]{2,1,0:T(8,128)(2,1)S(1)}, bf16[2,600,768]{2,1,0:T(8,128)(2,1)}, u32[]{:S(2)}) copy-start(bf16[2,600,768]{2,1,0:T(8,128)(2,1)} %param.35) | copy-start | bytes 5529604
  362.2 10.7 %copy-start.21 = (f32[1200]{0:T(1024)S(1)}, f32[1200]{0:T(1024)}, u32[]{:S(2)}) copy-start(f32[1200]{0:T(1024)} %reshape.395) | copy-start | bytes 14404
  372.9 5.2 copy-start.44
  381.3 252.3 %reduce-scatter.5.cloned.1.call-start = ((), (), s32[]{:S(2)}) async-start(), calls=%async_computation.7 | async-start | bytes 7299072 | tf_op jit(solution)/shard_map/reduce_scatter | solution.py:179
  386.3 116.0 %copy-start.20 = (f32[2,600]{1,0:T(2,128)S(1)}, f32[2,600]{1,0:T(2,128)}, u32[]{:S(2)}) copy-start(f32[2,600]{1,0:T(2,128)} %copy-done.19) | copy-start | bytes 14404
  386.3 116.0 %copy-start.26 = (f32[2,600]{1,0:T(2,128)S(1)}, f32[2,600]{1,0:T(2,128)}, u32[]{:S(2)}) copy-start(f32[2,600]{1,0:T(2,128)} %copy-done.25) | copy-start | bytes 14404
  386.3 116.0 %copy-start.28 = (f32[768]{0:T(1024)S(1)}, f32[768]{0:T(1024)}, u32[]{:S(2)}) copy-start(f32[768]{0:T(1024)} %copy-done.27) | copy-start | bytes 9220
  386.3 116.0 %copy-start.38 = (f32[768]{0:T(1024)S(1)}, f32[768]{0:T(1024)}, u32[]{:S(2)}) copy-start(f32[768]{0:T(1024)} %copy-done.37) | copy-start | bytes 9220
  514.1 260.8 %reduce-scatter.11.cloned.1.call-start = ((), (), s32[]{:S(2)}) async-start(), calls=%async_computation.10 | async-start | bytes 9732096 | tf_op jit(solution)/shard_map/reduce_scatter | solution.py:187
  529.1 387.8 %reduce-scatter.9.cloned.1.call-start = ((), (), s32[]{:S(2)}) async-start(), calls=%async_computation.9 | async-start | bytes 9732096 | tf_op jit(solution)/shard_map/reduce_scatter | solution.py:185
  557.1 10.7 %copy-start.31 = (f32[768]{0:T(1024)S(1)}, f32[768]{0:T(1024)}, u32[]{:S(2)}) copy-start(f32[768]{0:T(1024)} %get-tuple-element.180) | copy-start | bytes 9220
  557.1 10.7 %copy-start.32 = (f32[768]{0:T(1024)S(1)}, f32[768]{0:T(1024)}, u32[]{:S(2)}) copy-start(f32[768]{0:T(1024)} %get-tuple-element.178) | copy-start | bytes 9220
  557.1 10.7 %copy-start.34 = (f32[3072]{0:T(1024)S(1)}, f32[3072]{0:T(1024)}, u32[]{:S(2)}) copy-start(f32[3072]{0:T(1024)} %get-tuple-element.203) | copy-start | bytes 36868
  557.1 10.7 %copy-start.40 = (f32[768]{0:T(1024)S(1)}, f32[768]{0:T(1024)}, u32[]{:S(2)}) copy-start(f32[768]{0:T(1024)} %get-tuple-element.126) | copy-start | bytes 9220
  557.1 10.7 %copy-start.41 = (f32[768]{0:T(1024)S(1)}, f32[768]{0:T(1024)}, u32[]{:S(2)}) copy-start(f32[768]{0:T(1024)} %get-tuple-element.131) | copy-start | bytes 9220
  613.6 5.2 copy-start.5
  613.6 5.2 copy-start.22
  (20 other events, 48.1 us)
Sparse Core Ops, SparseCore 0:
  10.9 68.2 all-gather.3
  82.1 124.5 all-gather.5
  209.6 62.4 all-gather.7
  381.5 97.9 reduce-scatter.6
  514.2 119.3 reduce-scatter.4
  639.9 134.9 reduce-scatter.10
  782.4 134.4 reduce-scatter.8
